TPU v7x, 32 devices: a whole 2x2x4 slice. The times are simulated.
32 devices in a mesh: rows: 8 (over y, x, core), cols: 4 (over z).
Axes of the slice: x: 2, y: 2, z: 4, core: 2. Of those that a mesh axis runs over, the one named last changes fastest.
Arguments:
- snapshots: float32 [8192, 8192], P('rows', 'cols'), may hold values from -500 to 500, as said below
Outputs:
- updated: float32 [8192, 8192], P('rows', 'cols')
- coeffs: float32 [512, 8192], P(None, 'cols')
Inputs may be any that keep to these rules, and one draw needn't show every extreme that they name: `snapshots`: Real-valued entries.
All inputs are finite; a program needn't handle non-finite values.
Results may differ from a plain program's by a relative error of at most 0.000055.
Values sent between devices are 32-bit elements; how exact they have to be, the bound alone decides.
No kernel may reach another device: no remote copies, remote signals or barrier semaphores. Data moves between devices by JAX's collectives and lax.ppermute only.
A program may use at most 128 MiB of HBM per device.

v0:
```python
import jax
import jax.numpy as jnp
from jax import lax
from jax.sharding import PartitionSpec as P

PB = 512


def broadcast(block, axis, source):
    block = jnp.where(lax.axis_index(axis) == source, block, jnp.zeros_like(block))
    return lax.psum(block, axis)


def shards(snapshots):
    highest = lax.Precision.HIGHEST
    rows_dev, cols_dev = snapshots.shape
    total_rows = rows_dev * lax.axis_size("rows")
    panel = snapshots[:, :PB]
    local_gram = (
        jnp.dot(panel.T, panel, precision=highest, preferred_element_type=jnp.float32) / total_rows
    )
    gram = lax.psum(local_gram, "rows")
    lower = jnp.linalg.cholesky(gram)
    factor = lower.T
    basis = lax.linalg.triangular_solve(lower, panel, left_side=False, lower=True, transpose_a=True)
    basis = broadcast(basis, "cols", 0)
    partial_proj = (
        jnp.dot(basis.T, snapshots, precision=highest, preferred_element_type=jnp.float32)
        / total_rows
    )
    proj = lax.psum(partial_proj, "rows")
    column = lax.axis_index("cols") * cols_dev + jnp.arange(cols_dev, dtype=jnp.int32)
    is_panel = (column < PB)[None, :]
    coeff_fill = jnp.concatenate([factor, jnp.zeros((PB, cols_dev - PB), jnp.float32)], axis=1)
    coeffs = jnp.where(is_panel, coeff_fill, proj)
    trailing = snapshots - jnp.dot(
        basis, proj, precision=highest, preferred_element_type=jnp.float32
    )
    basis_fill = jnp.concatenate([basis, jnp.zeros((rows_dev, cols_dev - PB), jnp.float32)], axis=1)
    updated = jnp.where(is_panel, basis_fill, trailing)
    return (updated, coeffs)


def solution(mesh):
    in_specs = (P("rows", "cols"),)
    out_specs = (P("rows", "cols"), P(None, "cols"))
    return jax.shard_map(shards, mesh=mesh, in_specs=in_specs, out_specs=out_specs, check_vma=False)
```

profile of v0, /device:TPU:0, one launch (start us, length us, event | category | flops | bytes accessed | tf_op | source)
XLA Modules:
  0.0 450.0 jit_solution(13193877418435620194)
XLA Ops:
  7.2 6.7 %fusion.8 = f32[512,512]{0,1:T(8,128)} fusion(f32[1024,2048]{1,0:T(8,128)} %param.1), kind=kOutput, calls=%fused_computation.14 | convolution fusion | flops 3221487616 | bytes 3145728 | tf_op jit(solution)/shard_map/dot_general | solution.py:20
  14.2 59.2 %all-reduce.7.cloned.1.call-done = f32[512,512]{0,1:T(8,128)} async-done(((f32[512,512]{0,1:T(8,128)}), f32[512,512]{0,1:T(8,128)}) %all-reduce.7.cloned.1.call-update) | async-done | bytes 1048592 | tf_op jit(solution)/shard_map/psum | solution.py:22
  76.5 11.7 %cholesky.104 = f32[128,128]{1,0:T(8,128)S(1)} custom-call(f32[128,128]{1,0:T(8,128)S(1)} %cholesky.266), custom_call_target="Cholesky" | custom-call | tf_op jit(solution)/shard_map/jit(cholesky)/cholesky | solution.py:23
  88.2 9.8 %custom-call.30 = f32[1,128,128]{1,2,0:T(8,128)S(1)} custom-call(f32[1,128,128]{2,1,0:T(8,128)S(1)} %get-tuple-element.33), custom_call_target="InvertDiagBlocksLowerTriangular" | custom-call | tf_op jit(solution)/shard_map/jit(cholesky)/cholesky | solution.py:23
  98.8 11.7 %cholesky.217 = f32[128,128]{1,0:T(8,128)S(1)} custom-call(f32[128,128]{1,0:T(8,128)S(1)} %cholesky.270), custom_call_target="Cholesky" | custom-call | tf_op jit(solution)/shard_map/jit(cholesky)/cholesky | solution.py:23
  110.6 10.0 %custom-call.31 = f32[1,128,128]{1,2,0:T(8,128)S(1)} custom-call(f32[1,128,128]{2,1,0:T(8,128)S(1)} %get-tuple-element.30), custom_call_target="InvertDiagBlocksLowerTriangular" | custom-call | tf_op jit(solution)/shard_map/jit(cholesky)/cholesky | solution.py:23
  121.2 11.7 %cholesky.238 = f32[128,128]{1,0:T(8,128)S(1)} custom-call(f32[128,128]{1,0:T(8,128)S(1)} %cholesky.275), custom_call_target="Cholesky" | custom-call | tf_op jit(solution)/shard_map/jit(cholesky)/cholesky | solution.py:23
  133.7 9.8 %custom-call.32 = f32[1,128,128]{1,2,0:T(8,128)S(1)} custom-call(f32[1,128,128]{2,1,0:T(8,128)S(1)} %get-tuple-element.27), custom_call_target="InvertDiagBlocksLowerTriangular" | custom-call | tf_op jit(solution)/shard_map/jit(cholesky)/cholesky | solution.py:23
  144.1 11.7 %cholesky.255 = f32[128,128]{1,0:T(8,128)S(1)} custom-call(f32[128,128]{1,0:T(8,128)S(1)} %convolution_subtract_fusion.4), custom_call_target="Cholesky" | custom-call | tf_op jit(solution)/shard_map/jit(cholesky)/cholesky | solution.py:23
  160.4 8.5 %while.1 = (s32[]{:T(128)}, f32[512,512]{1,0:T(8,128)S(1)}, s32[4,2]{0,1:T(2,128)S(1)}, f32[4,128,128]{2,1,0:T(8,128)S(1)}, s32[]{:T(128)}) while((s32[]{:T(128)}, f32[512,512]{1,0:T(8,128)S(1)}, s32[4,2]{0,1:T(2,128)S(1)}, f32[4,128,128]{2,1,0:T(8,128)S(1)}, s32[]{:T(128)}) %tuple.33), condition=%wide.while_cond, body=%wide.while_body.sunk | while | flops 2 | bytes 131189 | solution.py:25
  168.9 39.3 %custom-call.33 = f32[4,128,128]{1,2,0:T(8,128)S(1)} custom-call(f32[4,128,128]{2,1,0:T(8,128)S(1)} %get-tuple-element.9), custom_call_target="InvertDiagBlocksLowerTriangular" | custom-call | tf_op jit(solution)/shard_map/triangular_solve | solution.py:25
  208.2 1.7 fusion.20
  209.9 2.0 convolution_subtract_fusion.1
  212.6 2.9 convolution_subtract_fusion
  216.1 3.8 fusion.11
  220.5 1.6 maximum_select_fusion
  222.3 85.5 %all-reduce.9.cloned.1.call-done = f32[1024,512]{0,1:T(8,128)} async-done(((f32[1024,512]{0,1:T(8,128)}), f32[1024,512]{0,1:T(8,128)}) %all-reduce.9.cloned.1.call-update) | async-done | bytes 2097168 | tf_op jit(solution)/shard_map/psum | solution.py:11
  307.8 17.7 %convolution_multiply_fusion = f32[512,2048]{0,1:T(8,128)} fusion(f32[1024,512]{0,1:T(8,128)} %all-reduce.9.cloned.1.call-done, f32[1024,2048]{1,0:T(8,128)} %param.1), kind=kOutput, calls=%fused_computation.4 | convolution fusion | flops 12885950464 | bytes 14680064 | tf_op jit(solution)/shard_map/dot_general | solution.py:28
  325.5 9.2 %copy.6 = f32[1024,2048]{0,1:T(8,128)} copy(f32[1024,2048]{1,0:T(8,128)} %param.1) | data formatting | bytes 16777216 | tf_op args[0]
  334.7 70.9 %all-reduce.11.cloned.1.call-done = f32[512,2048]{0,1:T(8,128)} async-done(((f32[512,2048]{0,1:T(8,128)}), f32[512,2048]{0,1:T(8,128)}) %all-reduce.11.cloned.1.call-update) | async-done | bytes 4194320 | tf_op jit(solution)/shard_map/psum | solution.py:31
  405.7 3.8 pad_select_fusion
  409.5 5.5 %copy.9 = f32[512,2048]{1,0:T(8,128)} copy(f32[512,2048]{0,1:T(8,128)} %pad_select_fusion) | data formatting | bytes 8388608
  414.9 19.2 %subtract_select_fusion = f32[1024,2048]{0,1:T(8,128)} fusion(f32[1024,2048]{0,1:T(8,128)} %copy.6, f32[1024,512]{0,1:T(8,128)S(1)} %copy-done, pred[2048]{0:T(1024)(128)(4,1)S(1)} %add_compare_fusion, f32[512,2048]{0,1:T(8,128)} %all-reduce.11.cloned.1.call-done), kind=kOutput, calls=%fused_computation.2 | convolution fusion | flops 12889096192 | bytes 23070720 | tf_op jit(solution)/shard_map/dot_general | solution.py:36
  434.1 9.1 %copy.8 = f32[1024,2048]{1,0:T(8,128)} copy(f32[1024,2048]{0,1:T(8,128)} %subtract_select_fusion) | data formatting | bytes 16777216
  (47 shorter events, 18.6 us)
Async XLA Ops:
  7.2 66.3 %all-reduce.7.cloned.1.call-start = ((), (), s32[]{:S(2)}) async-start(), calls=%async_computation | async-start | bytes 2097152 | tf_op jit(solution)/shard_map/psum | solution.py:22
  14.0 293.9 %all-reduce.9.cloned.1.call-start = ((), (), s32[]{:S(2)}) async-start(), calls=%async_computation.1 | async-start | bytes 4194304 | tf_op jit(solution)/shard_map/psum | solution.py:11
  222.1 183.5 %all-reduce.11.cloned.1.call-start = ((), (), s32[]{:S(2)}) async-start(), calls=%async_computation.2 | async-start | bytes 8388608 | tf_op jit(solution)/shard_map/psum | solution.py:31
  409.5 5.5 %copy-start = (f32[1024,512]{0,1:T(8,128)S(1)}, f32[1024,512]{0,1:T(8,128)}, u32[]{:S(2)}) copy-start(f32[1024,512]{0,1:T(8,128)} %all-reduce.9.cloned.1.call-done) | copy-start | bytes 6291460
Sparse Core Ops, SparseCore 0:
  14.1 59.3 all-reduce.6
  222.2 85.5 all-reduce.8
  325.7 79.9 all-reduce.10
where the time goes:
time: 454 us; the launch traced here: 450 us
  waiting for transfers between devices  216 us (48%)
  other arithmetic  125 us (28%)
  matrix products  57.7 us (13%)
  local copies, waits for them, and re-layouts  33.9 us (7%)
  between operations  16.7 us (4%)
    psum x1, waiting for transfers between devices, broadcast(): return lax.psum(block, axis)  85.5 us
    another operation x14, other arithmetic, shards(): lower = jnp.linalg.cholesky(gram)  78.6 us
    psum x1, waiting for transfers between devices, shards(): proj = lax.psum(partial_proj, 'rows')  70.9 us
    psum x1, waiting for transfers between devices, shards(): gram = lax.psum(local_gram, 'rows')  59.2 us
    another operation x2, other arithmetic, shards(): lax.linalg.triangular_solve(lower, panel, left_side=False, lower=True, tr...  39.3 us
    unnamed x5, local copies, waits for them, and re-layouts  23.8 us
    dot_general x1, matrix products, shards(): jnp.dot(basis, proj, precision=highest, preferred_element_type=jnp.float32)  19.2 us
    dot_general x1, matrix products, shards(): jnp.dot(basis.T, snapshots, precision=highest, preferred_element_type=jnp...  17.7 us
  transfers between devices with their start and end apart: 3, of which 3 were waited for; matrix products, arithmetic and copies ran while one was open for 2% of the time, Pallas kernels for 0%

commit v1 on v0

--- a/solution.py
+++ b/solution.py
@@ -4,6 +4,14 @@
 from jax.sharding import PartitionSpec as P
 
 PB = 512
+
+
+def added_up(x, axis):
+    count, summed = (lax.axis_size(axis), x)
+    for stride in [1 << k for k in range(count.bit_length() - 1)]:
+        route = [(i, i ^ stride) for i in range(count)]
+        summed = summed + lax.ppermute(summed, axis, route)
+    return summed
 
 
 def broadcast(block, axis, source):
@@ -28,7 +36,7 @@
         jnp.dot(basis.T, snapshots, precision=highest, preferred_element_type=jnp.float32)
         / total_rows
     )
-    proj = lax.psum(partial_proj, "rows")
+    proj = added_up(partial_proj, "rows")
     column = lax.axis_index("cols") * cols_dev + jnp.arange(cols_dev, dtype=jnp.int32)
     is_panel = (column < PB)[None, :]
     coeff_fill = jnp.concatenate([factor, jnp.zeros((PB, cols_dev - PB), jnp.float32)], axis=1)

time: 454 us -> 571 us (1.26)
  waiting for transfers between devices: 216 us -> 325 us
  other arithmetic: 125 us -> 131 us
    ppermute x0 -> x3, waiting for transfers between devices: none -> 180 us  [added_up(): summed = summed + lax.ppermute(summed, axis, route)]
    psum x1 -> x0, waiting for transfers between devices: 70.9 us -> none  [shards(): proj = lax.psum(partial_proj, 'rows')]
  transfers between devices with their start and end apart: 3 -> 5, of which waited for: 3 -> 5; matrix products, arithmetic and copies ran while one was open for 2% -> 2% of each run, Pallas kernels for 0% -> 0%
where the time goes in v1:
time: 571 us; the launch traced here: 567 us
  waiting for transfers between devices  325 us (57%)
  other arithmetic  131 us (23%)
  matrix products  57.1 us (10%)
  local copies, waits for them, and re-layouts  33.9 us (6%)
  between operations  17 us (3%)
    ppermute x3, waiting for transfers between devices, added_up(): summed = summed + lax.ppermute(summed, axis, route)  180 us
    psum x1, waiting for transfers between devices, broadcast(): return lax.psum(block, axis)  85.7 us
    another operation x14, other arithmetic, shards(): lower = jnp.linalg.cholesky(gram)  78.6 us
    psum x1, waiting for transfers between devices, shards(): gram = lax.psum(local_gram, 'rows')  59.2 us
    another operation x2, other arithmetic, shards(): lax.linalg.triangular_solve(lower, panel, left_side=False, lower=True, tr...  39.3 us
    unnamed x5, local copies, waits for them, and re-layouts  23.9 us
    dot_general x1, matrix products, shards(): jnp.dot(basis, proj, precision=highest, preferred_element_type=jnp.float32)  19.6 us
    dot_general x1, matrix products, shards(): jnp.dot(basis.T, snapshots, precision=highest, preferred_element_type=jnp...  16.6 us
  transfers between devices with their start and end apart: 5, of which 5 were waited for; matrix products, arithmetic and copies ran while one was open for 2% of the time, Pallas kernels for 0%

profile of v1, /device:TPU:0, one launch (start us, length us, event | category | flops | bytes accessed | tf_op | source)
XLA Modules:
  0.0 566.9 jit_solution(11015083892864941306)
XLA Ops:
  7.2 6.7 %fusion.9 = f32[512,512]{0,1:T(8,128)} fusion(f32[1024,2048]{1,0:T(8,128)} %param.1), kind=kOutput, calls=%fused_computation.15 | convolution fusion | flops 3221487616 | bytes 3145728 | tf_op jit(solution)/shard_map/dot_general | solution.py:28
  14.2 59.2 %all-reduce.6.cloned.1.call-done = f32[512,512]{0,1:T(8,128)} async-done(((f32[512,512]{0,1:T(8,128)}), f32[512,512]{0,1:T(8,128)}) %all-reduce.6.cloned.1.call-update) | async-done | bytes 1048592 | tf_op jit(solution)/shard_map/psum | solution.py:30
  76.5 11.7 %cholesky.104 = f32[128,128]{1,0:T(8,128)S(1)} custom-call(f32[128,128]{1,0:T(8,128)S(1)} %cholesky.266), custom_call_target="Cholesky" | custom-call | tf_op jit(solution)/shard_map/jit(cholesky)/cholesky | solution.py:31
  88.2 9.8 %custom-call.30 = f32[1,128,128]{1,2,0:T(8,128)S(1)} custom-call(f32[1,128,128]{2,1,0:T(8,128)S(1)} %get-tuple-element.33), custom_call_target="InvertDiagBlocksLowerTriangular" | custom-call | tf_op jit(solution)/shard_map/jit(cholesky)/cholesky | solution.py:31
  98.8 11.7 %cholesky.217 = f32[128,128]{1,0:T(8,128)S(1)} custom-call(f32[128,128]{1,0:T(8,128)S(1)} %cholesky.270), custom_call_target="Cholesky" | custom-call | tf_op jit(solution)/shard_map/jit(cholesky)/cholesky | solution.py:31
  110.6 10.0 %custom-call.31 = f32[1,128,128]{1,2,0:T(8,128)S(1)} custom-call(f32[1,128,128]{2,1,0:T(8,128)S(1)} %get-tuple-element.30), custom_call_target="InvertDiagBlocksLowerTriangular" | custom-call | tf_op jit(solution)/shard_map/jit(cholesky)/cholesky | solution.py:31
  121.2 11.7 %cholesky.238 = f32[128,128]{1,0:T(8,128)S(1)} custom-call(f32[128,128]{1,0:T(8,128)S(1)} %cholesky.275), custom_call_target="Cholesky" | custom-call | tf_op jit(solution)/shard_map/jit(cholesky)/cholesky | solution.py:31
  133.7 9.8 %custom-call.32 = f32[1,128,128]{1,2,0:T(8,128)S(1)} custom-call(f32[1,128,128]{2,1,0:T(8,128)S(1)} %get-tuple-element.27), custom_call_target="InvertDiagBlocksLowerTriangular" | custom-call | tf_op jit(solution)/shard_map/jit(cholesky)/cholesky | solution.py:31
  144.1 11.7 %cholesky.255 = f32[128,128]{1,0:T(8,128)S(1)} custom-call(f32[128,128]{1,0:T(8,128)S(1)} %convolution_subtract_fusion.4), custom_call_target="Cholesky" | custom-call | tf_op jit(solution)/shard_map/jit(cholesky)/cholesky | solution.py:31
  160.4 8.5 %while.1 = (s32[]{:T(128)}, f32[512,512]{1,0:T(8,128)S(1)}, s32[4,2]{0,1:T(2,128)S(1)}, f32[4,128,128]{2,1,0:T(8,128)S(1)}, s32[]{:T(128)}) while((s32[]{:T(128)}, f32[512,512]{1,0:T(8,128)S(1)}, s32[4,2]{0,1:T(2,128)S(1)}, f32[4,128,128]{2,1,0:T(8,128)S(1)}, s32[]{:T(128)}) %tuple.33), condition=%wide.while_cond, body=%wide.while_body.sunk | while | flops 2 | bytes 131189 | solution.py:33
  168.9 39.3 %custom-call.33 = f32[4,128,128]{1,2,0:T(8,128)S(1)} custom-call(f32[4,128,128]{2,1,0:T(8,128)S(1)} %get-tuple-element.9), custom_call_target="InvertDiagBlocksLowerTriangular" | custom-call | tf_op jit(solution)/shard_map/triangular_solve | solution.py:33
  212.6 2.9 convolution_subtract_fusion
  216.1 3.8 fusion.12
  222.1 85.7 %all-reduce.8.cloned.1.call-done = f32[1024,512]{0,1:T(8,128)} async-done(((f32[1024,512]{0,1:T(8,128)}), f32[1024,512]{0,1:T(8,128)}) %all-reduce.8.cloned.1.call-update) | async-done | bytes 2097168 | tf_op jit(solution)/shard_map/psum | solution.py:19
  307.8 16.6 %convolution_multiply_fusion = f32[512,2048]{0,1:T(8,128)S(1)} fusion(f32[1024,512]{0,1:T(8,128)} %all-reduce.8.cloned.1.call-done, f32[1024,2048]{1,0:T(8,128)} %param.1), kind=kOutput, calls=%fused_computation.4 | convolution fusion | flops 12885950464 | bytes 14680064 | tf_op jit(solution)/shard_map/dot_general | solution.py:36
  324.5 7.1 %collective-permute-done = f32[512,2048]{0,1:T(8,128)S(1)} collective-permute-done((f32[512,2048]{0,1:T(8,128)S(1)}, f32[512,2048]{0,1:T(8,128)S(1)}, u32[]{:S(2)}, u32[]{:S(2)}) %collective-permute-start) | collective-permute-done | bytes 4194336 | tf_op jit(solution)/shard_map/ppermute | solution.py:13
  334.2 91.1 %collective-permute-done.1 = f32[512,2048]{0,1:T(8,128)S(1)} collective-permute-done((f32[512,2048]{0,1:T(8,128)S(1)}, f32[512,2048]{0,1:T(8,128)S(1)}, u32[]{:S(2)}, u32[]{:S(2)}) %collective-permute-start.1) | collective-permute-done | bytes 4194336 | tf_op jit(solution)/shard_map/ppermute | solution.py:13
  425.3 3.0 add.71
  429.8 9.2 %copy.6 = f32[1024,2048]{0,1:T(8,128)} copy(f32[1024,2048]{1,0:T(8,128)} %param.1) | data formatting | bytes 16777216 | tf_op args[0]
  439.0 81.4 %collective-permute-done.2 = f32[512,2048]{0,1:T(8,128)} collective-permute-done((f32[512,2048]{0,1:T(8,128)}, f32[512,2048]{0,1:T(8,128)}, u32[]{:S(2)}, u32[]{:S(2)}) %collective-permute-start.2) | collective-permute-done | bytes 4194336 | tf_op jit(solution)/shard_map/ppermute | solution.py:13
  520.4 5.1 pad_select_fusion
  525.5 5.5 copy.9
  531.0 19.6 %subtract_select_fusion = f32[1024,2048]{0,1:T(8,128)} fusion(f32[1024,2048]{0,1:T(8,128)} %copy.6, f32[1024,512]{0,1:T(8,128)S(1)} %copy-done, pred[2048]{0:T(1024)(128)(4,1)S(1)} %add_compare_fusion, f32[512,2048]{0,1:T(8,128)} %add.71, f32[512,2048]{0,1:T(8,128)} %collective-permute-done.2), kind=kOutput, calls=%fused_computation.2 | convolution fusion | flops 12890144768 | bytes 27265024 | tf_op jit(solution)/shard_map/dot_general | solution.py:44
  550.7 9.1 %copy.8 = f32[1024,2048]{1,0:T(8,128)} copy(f32[1024,2048]{0,1:T(8,128)} %subtract_select_fusion) | data formatting | bytes 16777216
  (52 shorter events, 27.8 us)
Async XLA Ops:
  7.2 66.3 %all-reduce.6.cloned.1.call-start = ((), (), s32[]{:S(2)}) async-start(), calls=%async_computation | async-start | bytes 2097152 | tf_op jit(solution)/shard_map/psum | solution.py:30
  14.0 293.9 %all-reduce.8.cloned.1.call-start = ((), (), s32[]{:S(2)}) async-start(), calls=%async_computation.1 | async-start | bytes 4194304 | tf_op jit(solution)/shard_map/psum | solution.py:19
  324.4 7.2 %collective-permute-start = (f32[512,2048]{0,1:T(8,128)S(1)}, f32[512,2048]{0,1:T(8,128)S(1)}, u32[]{:S(2)}, u32[]{:S(2)}) collective-permute-start(f32[512,2048]{0,1:T(8,128)S(1)} %convolution_multiply_fusion), channel_id=1, source_target_pairs={{0,4},{4,0},{8,12},{12,8},{16,20},{20,16},{24,28},{28,24},{1,5},{5... | collective-permute-start | bytes 12582920 | tf_op jit(solution)/shard_map/ppermute | solution.py:13
  332.6 92.7 %collective-permute-start.1 = (f32[512,2048]{0,1:T(8,128)S(1)}, f32[512,2048]{0,1:T(8,128)S(1)}, u32[]{:S(2)}, u32[]{:S(2)}) collective-permute-start(f32[512,2048]{0,1:T(8,128)S(1)} %add.70), channel_id=1, source_target_pairs={{0,8},{4,12},{8,0},{12,4},{16,24},{20,28},{24,16},{28,20},{1,9},{5... | collective-permute-start | bytes 12582920 | tf_op jit(solution)/shard_map/ppermute | solution.py:13
  428.3 92.1 %collective-permute-start.2 = (f32[512,2048]{0,1:T(8,128)}, f32[512,2048]{0,1:T(8,128)}, u32[]{:S(2)}, u32[]{:S(2)}) collective-permute-start(f32[512,2048]{0,1:T(8,128)} %add.71), channel_id=1, source_target_pairs={{0,16},{4,20},{8,24},{12,28},{16,0},{20,4},{24,8},{28,12},{1,17},{... | collective-permute-start | bytes 12582920 | tf_op jit(solution)/shard_map/ppermute | solution.py:13
  525.5 5.5 copy-start
Sparse Core Ops, SparseCore 0:
  14.1 59.3 all-reduce.5
  222.2 85.5 all-reduce.7
